TPU v7x, 32 devices: a whole 2x2x4 slice. The times are simulated.
32 devices in a mesh: dom: 8 (over z, core), four: 4 (over y, x).
Axes of the slice: x: 2, y: 2, z: 4, core: 2. Of those that a mesh axis runs over, the one named last changes fastest.
Arguments:
- velocity: float32 [3, 128, 18432], P(None, 'four', 'dom'), may hold values from -16 to 16
- partner: int32 [8, 4], P('dom'), may hold values from -1 to 7, as said below
- partner_side: int32 [8, 4], P('dom'), may hold values from -1 to 3, as said below
- flipped: int32 [8, 4], P('dom'), may hold values from 0 to 1, as said below
Outputs:
- new_velocity: float32 [3, 128, 18432], P(None, 'four', 'dom')
- residual: float32 [3, 128, 18432], P(None, 'four', 'dom')
Inputs may be any that keep to these rules, and one draw needn't show every extreme that they name: `partner`: sides are numbered 0 bottom, 1 right, 2 top, 3 left. Gluing is symmetric: if side s of partition p is glued to side s2 of partition q, then side s2 of q is glued to side s of p with the same flipped value. No side is glued to itself, and exactly 4 sides are walls (-1). `partner_side`: -1 exactly where partner is -1. `flipped`: 0 on wall sides.
All inputs are finite; a program needn't handle non-finite values.
Results may differ from a plain program's by a relative error of at most 0.0003.
Values sent between devices are 32-bit elements; how exact they have to be, the bound alone decides.
No kernel may reach another device: no remote copies, remote signals or barrier semaphores. Data moves between devices by JAX's collectives and lax.ppermute only.
A program may use at most 128 MiB of HBM per device.

v0:
```python
import math
import jax
import jax.numpy as jnp
import numpy as np
from jax import lax
from jax.sharding import PartitionSpec as P

ITERS = 4
REACTION = 2.0
WAVE_STEP = 0.0625
HIGHEST = lax.Precision.HIGHEST


def gll_tables():
    inner_near = math.sqrt(1.0 / 3.0 - 2.0 * math.sqrt(7.0) / 21.0)
    inner_far = math.sqrt(1.0 / 3.0 + 2.0 * math.sqrt(7.0) / 21.0)
    points = np.array([-1.0, -inner_far, -inner_near, inner_near, inner_far, 1.0])
    values = (63.0 * points**5 - 70.0 * points**3 + 15.0 * points) / 8.0
    weights = 2.0 / (30.0 * values * values)
    spacing = points[:, None] - points[None, :]
    same_point = spacing == 0.0
    derivative = np.where(
        same_point, 0.0, values[:, None] / (values[None, :] * np.where(same_point, 1.0, spacing))
    )
    end_fix = np.array([-7.5, 0.0, 0.0, 0.0, 0.0, 7.5])
    derivative = derivative + np.eye(6) * end_fix[None, :]
    stiffness = derivative.T @ (weights[:, None] * derivative)
    return (weights, derivative, stiffness)


def block_tables(blocks):
    weights, derivative, stiffness = gll_tables()
    identity = np.eye(blocks)
    weights_line = jnp.asarray(np.tile(weights, blocks), dtype=jnp.float32)
    deriv_block = jnp.asarray(np.kron(identity, derivative), dtype=jnp.float32)
    stiff_block = jnp.asarray(np.kron(identity, stiffness), dtype=jnp.float32)
    return (weights_line, deriv_block, stiff_block)


def fourier_tables(planes):
    plane_ids = jnp.arange(planes, dtype=jnp.int32)
    mode_ids = jnp.arange(planes, dtype=jnp.int32)
    waves = jnp.where(mode_ids < 2, 0, mode_ids // 2)
    phase_index = plane_ids[:, None] * waves[None, :] % planes
    angle = phase_index.astype(jnp.float32) * (2.0 * math.pi / planes)
    is_sine = (mode_ids % 2 == 1) & (mode_ids >= 2)
    basis = jnp.where(is_sine[None, :], jnp.sin(angle), jnp.cos(angle))
    alternating = jnp.where(plane_ids % 2 == 0, 1.0, -1.0).astype(jnp.float32)
    basis = jnp.where(mode_ids[None, :] == 1, alternating[:, None], basis)
    row_scale = jnp.where(mode_ids < 2, 1.0, 2.0).astype(jnp.float32) / planes
    forward = basis.T * row_scale[:, None]
    return (basis, forward)


def helmholtz_rates(mode_ids, planes):
    waves = jnp.where(mode_ids == 0, 0, jnp.where(mode_ids == 1, planes // 2, mode_ids // 2))
    scaled = waves.astype(jnp.float32) * WAVE_STEP
    return REACTION + scaled * scaled


def z_derivative(fields, mode_ids):
    waves = (mode_ids[0::2] // 2).astype(jnp.float32) * WAVE_STEP
    paired = fields.reshape(fields.shape[:1] + (-1, 2) + fields.shape[2:])
    cosine = paired[:, :, 0]
    sine = paired[:, :, 1]
    pair_waves = waves[None, :, None, None]
    result = jnp.stack([pair_waves * sine, -pair_waves * cosine], axis=2)
    return result.reshape(fields.shape)


def nonlinear_term(grids, mode_ids, deriv_block):
    along_x = jnp.matmul(grids[0:3], deriv_block.T, precision=HIGHEST)
    along_y = jnp.matmul(deriv_block, jnp.stack([grids[1], grids[3], grids[4]]), precision=HIGHEST)
    along_z = z_derivative(jnp.stack([grids[2], grids[4], grids[5]]), mode_ids)
    return -(along_x + along_y + along_z)


def pair_products(physical):
    return jnp.stack(
        [
            physical[0] * physical[0],
            physical[0] * physical[1],
            physical[0] * physical[2],
            physical[1] * physical[1],
            physical[1] * physical[2],
            physical[2] * physical[2],
        ]
    )


def junction_flags(side_nodes):
    positions = jnp.arange(side_nodes)
    at_end = (positions % 6 == 5) & (positions < side_nodes - 1)
    at_start = (positions % 6 == 0) & (positions > 0)
    return (at_end, at_start)


def dss_local(field):
    side_nodes = field.shape[-1]
    at_end, at_start = junction_flags(side_nodes)
    zero_col = jnp.zeros(field.shape[:-1] + (1,), field.dtype)
    from_right = jnp.concatenate([field[..., 1:], zero_col], axis=-1)
    from_left = jnp.concatenate([zero_col, field[..., :-1]], axis=-1)
    field = field + jnp.where(at_end, from_right, 0.0) + jnp.where(at_start, from_left, 0.0)
    zero_row = jnp.zeros(field.shape[:-2] + (1, side_nodes), field.dtype)
    from_below = jnp.concatenate([field[..., 1:, :], zero_row], axis=-2)
    from_above = jnp.concatenate([zero_row, field[..., :-1, :]], axis=-2)
    field = (
        field
        + jnp.where(at_end[:, None], from_below, 0.0)
        + jnp.where(at_start[:, None], from_above, 0.0)
    )
    return field


def side_values(grid):
    return jnp.stack(
        [grid[..., 0, :], grid[..., :, -1], grid[..., -1, :], grid[..., :, 0]], axis=-2
    )


def add_sides(grid, incoming):
    grid = grid.at[..., 0, :].add(incoming[..., 0, :])
    grid = grid.at[..., :, -1].add(incoming[..., 1, :])
    grid = grid.at[..., -1, :].add(incoming[..., 2, :])
    grid = grid.at[..., :, 0].add(incoming[..., 3, :])
    return grid


def edge_tables(partner_rows, side_nodes):
    positions = jnp.arange(side_nodes)
    rows_at = jnp.broadcast_to(positions[:, None], (side_nodes, side_nodes))
    cols_at = jnp.broadcast_to(positions[None, :], (side_nodes, side_nodes))
    on_side = jnp.stack(
        [rows_at == 0, cols_at == side_nodes - 1, rows_at == side_nodes - 1, cols_at == 0]
    )
    is_glued = (partner_rows >= 0)[..., :, None, None]
    wall_node = jnp.any(on_side & jnp.logical_not(is_glued), axis=-3)
    glued_node = jnp.any(on_side & is_glued, axis=-3)
    corner = ((rows_at == 0) | (rows_at == side_nodes - 1)) & (
        (cols_at == 0) | (cols_at == side_nodes - 1)
    )
    kept_node = jnp.logical_not(wall_node | corner)
    dirichlet_mask = kept_node.astype(jnp.float32)
    at_end, at_start = junction_flags(side_nodes)
    copies = jnp.where(at_end | at_start, 2.0, 1.0).astype(jnp.float32)
    weight = dirichlet_mask / (copies[:, None] * copies[None, :] * jnp.where(glued_node, 2.0, 1.0))
    return (dirichlet_mask, weight)


def apply_element(field, rates, weights_line, stiff_block):
    rows_part = jnp.matmul(stiff_block, field, precision=HIGHEST) * weights_line[None, :]
    cols_part = jnp.matmul(field, stiff_block, precision=HIGHEST) * weights_line[:, None]
    return rows_part + cols_part + rates * (weights_line[:, None] * weights_line[None, :]) * field


def inner_terms(weight, first_field, second_field):
    return jnp.sum(weight * first_field * second_field, axis=(-2, -1))


def shards(velocity, partner, partner_side, flipped):
    modes_here = velocity.shape[1]
    side_nodes = math.isqrt(velocity.shape[2])
    blocks = side_nodes // 6
    planes_all = modes_here * lax.axis_size("four")
    weights_line, deriv_block, stiff_block = block_tables(blocks)
    basis, forward = fourier_tables(planes_all)
    mode_ids = lax.axis_index("four") * modes_here + jnp.arange(modes_here, dtype=jnp.int32)
    mass_grid = weights_line[:, None] * weights_line[None, :]
    spread = lax.all_to_all(velocity, "four", split_axis=2, concat_axis=1, tiled=True)
    physical = jnp.einsum("jm,cmn->cjn", basis, spread, precision=HIGHEST)
    modal = jnp.einsum("mj,cjn->cmn", forward, pair_products(physical), precision=HIGHEST)
    returned = lax.all_to_all(modal, "four", split_axis=1, concat_axis=2, tiled=True)
    grids = returned.reshape(6, modes_here, side_nodes, side_nodes)
    nonlinear = nonlinear_term(grids, mode_ids, deriv_block)
    current = velocity.reshape(3, modes_here, side_nodes, side_nodes)
    local_rhs = mass_grid * (REACTION * current + nonlinear)
    partner_row = partner[0]
    side_row = partner_side[0]
    flip_row = flipped[0]
    dirichlet_mask, weight = edge_tables(partner, side_nodes)
    rates = helmholtz_rates(mode_ids, planes_all)[:, None, None]

    def assemble(field):
        joined = dss_local(field)
        edges = side_values(joined)
        leading = edges.shape[:2]
        packed = edges.reshape((1,) + leading + (4 * side_nodes,))
        piece = lax.all_gather(packed, "dom", axis=0, tiled=True)
        row_count = piece.shape[0]
        collected = []
        for side_index in range(4):
            offset_row = partner_row[side_index]
            inside = (offset_row >= 0) & (offset_row < row_count)
            chosen = lax.dynamic_index_in_dim(
                piece, jnp.clip(offset_row, 0, row_count - 1), 0, keepdims=False
            )
            segment = lax.dynamic_slice_in_dim(
                chosen, jnp.maximum(side_row[side_index], 0) * side_nodes, side_nodes, axis=2
            )
            segment = jnp.where(flip_row[side_index] == 1, segment[..., ::-1], segment)
            collected.append(jnp.where(inside, segment, 0.0))
        incoming = jnp.zeros(edges.shape, jnp.float32) + jnp.stack(collected, axis=2)
        return add_sides(joined, incoming)

    def operate(field):
        return dirichlet_mask * assemble(apply_element(field, rates, weights_line, stiff_block))

    def squares(residual):
        return lax.psum(inner_terms(weight, residual, residual), "dom")[..., None, None]

    def solve(rhs):
        solution = jnp.zeros_like(rhs)
        residual = rhs
        direction = rhs
        norm_now = squares(residual)
        for iteration in range(ITERS):
            image = operate(direction)
            alpha = (
                norm_now / lax.psum(inner_terms(weight, direction, image), "dom")[..., None, None]
            )
            solution = solution + alpha * direction
            residual = residual - alpha * image
            norm_next = squares(residual)
            direction = residual + norm_next / norm_now * direction
            norm_now = norm_next
        return (solution, residual)

    rhs_all = dirichlet_mask * assemble(local_rhs)
    results_each = [solve(rhs_all[component : component + 1]) for component in range(3)]
    solution = jnp.concatenate([outcome[0] for outcome in results_each], axis=0)
    residual = jnp.concatenate([outcome[1] for outcome in results_each], axis=0)
    new_velocity = solution.reshape(3, modes_here, side_nodes * side_nodes)
    return (new_velocity, residual.reshape(3, modes_here, side_nodes * side_nodes))


def solution(mesh):
    return jax.shard_map(
        shards,
        mesh=mesh,
        in_specs=(P(None, "four", "dom"), P("dom", None), P("dom", None), P("dom", None)),
        out_specs=(P(None, "four", "dom"), P(None, "four", "dom")),
        check_vma=False,
    )
```

profile of v0, /device:TPU:0, one launch (start us, length us, event | category | flops | bytes accessed | tf_op | source)
XLA Modules:
  0.0 1019.5 jit_solution(3872231014934521346)
XLA Ops:
  0.6 4.7 copy.6838
  5.3 5.6 reshape.2898
  10.9 5.2 all-to-all-start
  35.5 5.1 reshape.2899
  50.6 4.4 all-to-all-start.1
  63.8 21.1 %all-to-all-done.1 = f32[6,128,576]{2,0,1:T(8,128)S(1)} async-done(((f32[6,128,576]{2,0,1:T(8,128)}), f32[6,128,576]{2,0,1:T(8,128)S(1)}, u32[]{:S(2)}, u32[]{:S(2)}) %all-to-all-start.1) | async-done | bytes 1769504 | tf_op jit(solution)/shard_map/all_to_all | solution.py:173
  112.2 8.1 fusion.218
  135.2 15.8 %all_gather.39 = f32[8,3,32,192]{3,2,1,0:T(8,128)S(1)} all-gather(f32[1,3,32,192]{3,2,1,0:T(8,128)S(1)} %reshape.2780), channel_id=1, replica_groups=mesh['dom'=8,'four'=4] {'dom'}, dimensions={0}, use_global_device_ids=true | all-gather | bytes 663552 | tf_op jit(solution)/shard_map/all_gather | solution.py:189
  153.8 13.0 %scatter-add.174 = f32[3,32,48,48]{2,3,1,0:T(8,128)S(1)} dynamic-update-slice(f32[3,32,48,48]{2,3,1,0:T(8,128)S(1)} %select_add_fusion, f32[3,32,1,48]{2,3,1,0:T(8,128)} %copy.6860, s32[]{:T(128)} %constant.2451.clone.1, s32[]{:T(128)} %constant.2451.clone.1, s32[]{:T(128)} %constant.2451.clone.1, s32[]{:T(128)} %constant.2451.clone.1) | dynamic-update-slice | bytes 36868 | tf_op jit(solution)/shard_map/scatter-add | solution.py:123
  176.3 19.5 %scatter-add.176 = f32[3,32,48,48]{2,3,1,0:T(8,128)S(1)} dynamic-update-slice(f32[3,32,48,48]{2,3,1,0:T(8,128)S(1)} %scatter-add.175, f32[3,32,1,48]{2,3,1,0:T(8,128)} %copy.6864, s32[]{:T(128)} %constant.2451.clone.1, s32[]{:T(128)} %constant.2451.clone.1, s32[]{:T(128)} %constant.2452.clone.1, s32[]{:T(128)} %constant.2451.clone.1) | dynamic-update-slice | bytes 36868 | tf_op jit(solution)/shard_map/scatter-add | solution.py:125
  216.8 14.4 %all_gather.40 = f32[8,1,32,192]{3,2,1,0:T(8,128)S(1)} all-gather(f32[1,1,32,192]{3,2,1,0:T(8,128)S(1)} %reshape.2786), channel_id=1, replica_groups=mesh['dom'=8,'four'=4] {'dom'}, dimensions={0}, use_global_device_ids=true | all-gather | bytes 221184 | tf_op jit(solution)/shard_map/all_gather | solution.py:189
  241.6 5.3 scatter-add.184
  247.5 17.0 %all-reduce.57 = (f32[1,32]{1,0:T(1,128)S(1)}, f32[1,32]{1,0:T(1,128)S(1)}) all-reduce(f32[1,32]{1,0:T(1,128)S(1)} %bitcast.716, f32[1,32]{1,0:T(1,128)S(1)} %bitcast.715), channel_id=1, replica_groups=mesh['dom'=8,'four'=4] {'dom'}, use_global_device_ids=true, to_apply=%region_3.4 | all-reduce | flops 64 | bytes 512 | tf_op jit(solution)/shard_map/psum | solution.py:210
  265.0 13.6 %psum.170 = f32[1,32]{1,0:T(1,128)S(1)} all-reduce(f32[1,32]{1,0:T(1,128)S(1)} %bitcast.723), channel_id=1, replica_groups=mesh['dom'=8,'four'=4] {'dom'}, use_global_device_ids=true, to_apply=%region_7.8 | all-reduce | flops 32 | bytes 256 | tf_op jit(solution)/shard_map/psum | solution.py:210
  303.4 14.2 %all_gather.41 = f32[8,1,32,192]{3,2,1,0:T(8,128)S(1)} all-gather(f32[1,1,32,192]{3,2,1,0:T(8,128)S(1)} %reshape.2792), channel_id=1, replica_groups=mesh['dom'=8,'four'=4] {'dom'}, dimensions={0}, use_global_device_ids=true | all-gather | bytes 221184 | tf_op jit(solution)/shard_map/all_gather | solution.py:189
  330.5 5.8 scatter-add.190
  341.4 14.2 %all_gather.44 = f32[8,1,32,192]{3,2,1,0:T(8,128)S(1)} all-gather(f32[1,1,32,192]{3,2,1,0:T(8,128)S(1)} %reshape.2810), channel_id=1, replica_groups=mesh['dom'=8,'four'=4] {'dom'}, dimensions={0}, use_global_device_ids=true | all-gather | bytes 221184 | tf_op jit(solution)/shard_map/all_gather | solution.py:189
  366.1 5.3 scatter-add.210
  374.7 13.9 %psum.171 = f32[1,32]{1,0:T(1,128)S(1)} all-reduce(f32[1,32]{1,0:T(1,128)S(1)} %bitcast.719), channel_id=1, replica_groups=mesh['dom'=8,'four'=4] {'dom'}, use_global_device_ids=true, to_apply=%region_9.10 | all-reduce | flops 32 | bytes 256 | tf_op jit(solution)/shard_map/psum | solution.py:220
  391.2 14.0 %psum.172 = f32[1,32]{1,0:T(1,128)S(1)} all-reduce(f32[1,32]{1,0:T(1,128)S(1)} %bitcast.717), channel_id=1, replica_groups=mesh['dom'=8,'four'=4] {'dom'}, use_global_device_ids=true, to_apply=%region_11.12 | all-reduce | flops 32 | bytes 256 | tf_op jit(solution)/shard_map/psum | solution.py:210
  426.3 14.2 %all_gather.48 = f32[8,1,32,192]{3,2,1,0:T(8,128)S(1)} all-gather(f32[1,1,32,192]{3,2,1,0:T(8,128)S(1)} %reshape.2834), channel_id=1, replica_groups=mesh['dom'=8,'four'=4] {'dom'}, dimensions={0}, use_global_device_ids=true | all-gather | bytes 221184 | tf_op jit(solution)/shard_map/all_gather | solution.py:189
  453.8 5.8 scatter-add.236
  464.7 14.2 %all_gather.42 = f32[8,1,32,192]{3,2,1,0:T(8,128)S(1)} all-gather(f32[1,1,32,192]{3,2,1,0:T(8,128)S(1)} %reshape.2798), channel_id=1, replica_groups=mesh['dom'=8,'four'=4] {'dom'}, dimensions={0}, use_global_device_ids=true | all-gather | bytes 221184 | tf_op jit(solution)/shard_map/all_gather | solution.py:189
  489.3 5.3 scatter-add.196
  498.2 13.9 %all-reduce.56 = (f32[1,32]{1,0:T(1,128)S(1)}, f32[1,32]{1,0:T(1,128)S(1)}, f32[1,32]{1,0:T(1,128)S(1)}) all-reduce(f32[1,32]{1,0:T(1,128)S(1)} %bitcast.712, f32[1,32]{1,0:T(1,128)S(1)} %bitcast.711, f32[1,32]{1,0:T(1,128)S(1)} %bitcast.713), channel_id=1, replica_groups=mesh['dom'=8,'four'=4] {'dom'}, use_global_device_ids=true, to_apply=%region_35.36 | all-reduce | flops 96 | bytes 768 | tf_op jit(solution)/shard_map/psum | solution.py:210
  515.5 13.8 %all-reduce.55 = (f32[1,32]{1,0:T(1,128)S(1)}, f32[1,32]{1,0:T(1,128)S(1)}, f32[1,32]{1,0:T(1,128)S(1)}, f32[1,32]{1,0:T(1,128)S(1)}) all-reduce(f32[1,32]{1,0:T(1,128)S(1)} %bitcast.704, f32[1,32]{1,0:T(1,128)S(1)} %bitcast.703, f32[1,32]{1,0:T(1,128)S(1)} %bitcast.702, ...), channel_id=1, replica_groups=mesh['dom'=8,'four'=4] {'dom'}, use_global_device_ids=true, to_apply=%region_39.40 | all-reduce | flops 128 | bytes 1024 | tf_op jit(solution)/shard_map/psum | solution.py:210
  554.6 14.6 %all_gather.49 = f32[8,1,32,192]{3,2,1,0:T(8,128)S(1)} all-gather(f32[1,1,32,192]{3,2,1,0:T(8,128)S(1)} %reshape.2840), channel_id=1, replica_groups=mesh['dom'=8,'four'=4] {'dom'}, dimensions={0}, use_global_device_ids=true | all-gather | bytes 221184 | tf_op jit(solution)/shard_map/all_gather | solution.py:189
  582.3 5.8 scatter-add.244
  593.3 14.2 %all_gather.43 = f32[8,1,32,192]{3,2,1,0:T(8,128)S(1)} all-gather(f32[1,1,32,192]{3,2,1,0:T(8,128)S(1)} %reshape.2804), channel_id=1, replica_groups=mesh['dom'=8,'four'=4] {'dom'}, dimensions={0}, use_global_device_ids=true | all-gather | bytes 221184 | tf_op jit(solution)/shard_map/all_gather | solution.py:189
  618.1 5.3 scatter-add.204
  627.3 14.1 %psum.178 = f32[1,32]{1,0:T(1,128)S(1)} all-reduce(f32[1,32]{1,0:T(1,128)S(1)} %bitcast.720), channel_id=1, replica_groups=mesh['dom'=8,'four'=4] {'dom'}, use_global_device_ids=true, to_apply=%region_23.24 | all-reduce | flops 32 | bytes 256 | tf_op jit(solution)/shard_map/psum | solution.py:210
  656.8 14.2 %all_gather.45 = f32[8,1,32,192]{3,2,1,0:T(8,128)S(1)} all-gather(f32[1,1,32,192]{3,2,1,0:T(8,128)S(1)} %reshape.2816), channel_id=1, replica_groups=mesh['dom'=8,'four'=4] {'dom'}, dimensions={0}, use_global_device_ids=true | all-gather | bytes 221184 | tf_op jit(solution)/shard_map/all_gather | solution.py:189
  684.2 5.8 scatter-add.216
  693.0 13.9 %psum.179 = f32[1,32]{1,0:T(1,128)S(1)} all-reduce(f32[1,32]{1,0:T(1,128)S(1)} %bitcast.724), channel_id=1, replica_groups=mesh['dom'=8,'four'=4] {'dom'}, use_global_device_ids=true, to_apply=%region_25.26 | all-reduce | flops 32 | bytes 256 | tf_op jit(solution)/shard_map/psum | solution.py:220
  709.6 13.8 %psum.180 = f32[1,32]{1,0:T(1,128)S(1)} all-reduce(f32[1,32]{1,0:T(1,128)S(1)} %bitcast.718), channel_id=1, replica_groups=mesh['dom'=8,'four'=4] {'dom'}, use_global_device_ids=true, to_apply=%region_27.28 | all-reduce | flops 32 | bytes 256 | tf_op jit(solution)/shard_map/psum | solution.py:210
  741.0 14.2 %all_gather.46 = f32[8,1,32,192]{3,2,1,0:T(8,128)S(1)} all-gather(f32[1,1,32,192]{3,2,1,0:T(8,128)S(1)} %reshape.2822), channel_id=1, replica_groups=mesh['dom'=8,'four'=4] {'dom'}, dimensions={0}, use_global_device_ids=true | all-gather | bytes 221184 | tf_op jit(solution)/shard_map/all_gather | solution.py:189
  767.2 5.8 scatter-add.224
  776.1 13.9 %all-reduce.54 = (f32[1,32]{1,0:T(1,128)S(1)}, f32[1,32]{1,0:T(1,128)S(1)}) all-reduce(f32[1,32]{1,0:T(1,128)S(1)} %bitcast.706, f32[1,32]{1,0:T(1,128)S(1)} %bitcast.721), channel_id=1, replica_groups=mesh['dom'=8,'four'=4] {'dom'}, use_global_device_ids=true, to_apply=%region_41.42 | all-reduce | flops 64 | bytes 512 | tf_op jit(solution)/shard_map/psum | solution.py:220
  793.4 14.1 %all-reduce.53 = (f32[1,32]{1,0:T(1,128)S(1)}, f32[1,32]{1,0:T(1,128)S(1)}) all-reduce(f32[1,32]{1,0:T(1,128)S(1)} %bitcast.709, f32[1,32]{1,0:T(1,128)S(1)} %bitcast.708), channel_id=1, replica_groups=mesh['dom'=8,'four'=4] {'dom'}, use_global_device_ids=true, to_apply=%region_43.44 | all-reduce | flops 64 | bytes 512 | tf_op jit(solution)/shard_map/psum | solution.py:210
  832.3 14.2 %all_gather.50 = f32[8,1,32,192]{3,2,1,0:T(8,128)S(1)} all-gather(f32[1,1,32,192]{3,2,1,0:T(8,128)S(1)} %reshape.2846), channel_id=1, replica_groups=mesh['dom'=8,'four'=4] {'dom'}, dimensions={0}, use_global_device_ids=true | all-gather | bytes 221184 | tf_op jit(solution)/shard_map/all_gather | solution.py:189
  859.6 5.8 scatter-add.250
  871.8 14.2 %all_gather.47 = f32[8,1,32,192]{3,2,1,0:T(8,128)S(1)} all-gather(f32[1,1,32,192]{3,2,1,0:T(8,128)S(1)} %reshape.2828), channel_id=1, replica_groups=mesh['dom'=8,'four'=4] {'dom'}, dimensions={0}, use_global_device_ids=true | all-gather | bytes 221184 | tf_op jit(solution)/shard_map/all_gather | solution.py:189
  898.5 4.8 scatter-add.230
  909.7 13.9 %psum.189 = f32[1,32]{1,0:T(1,128)S(1)} all-reduce(f32[1,32]{1,0:T(1,128)S(1)} %bitcast.722), channel_id=1, replica_groups=mesh['dom'=8,'four'=4] {'dom'}, use_global_device_ids=true, to_apply=%region_45.46 | all-reduce | flops 32 | bytes 256 | tf_op jit(solution)/shard_map/psum | solution.py:220
  928.0 13.8 %psum.190 = f32[1,32]{1,0:T(1,128)S(1)} all-reduce(f32[1,32]{1,0:T(1,128)S(1)} %bitcast.714), channel_id=1, replica_groups=mesh['dom'=8,'four'=4] {'dom'}, use_global_device_ids=true, to_apply=%region_47.48 | all-reduce | flops 32 | bytes 256 | tf_op jit(solution)/shard_map/psum | solution.py:210
  955.5 14.2 %all_gather.51 = f32[8,1,32,192]{3,2,1,0:T(8,128)S(1)} all-gather(f32[1,1,32,192]{3,2,1,0:T(8,128)S(1)} %reshape.2852), channel_id=1, replica_groups=mesh['dom'=8,'four'=4] {'dom'}, dimensions={0}, use_global_device_ids=true | all-gather | bytes 221184 | tf_op jit(solution)/shard_map/all_gather | solution.py:189
  978.0 5.3 scatter-add.256
  985.2 14.2 %all-reduce.52 = (f32[1,32]{1,0:T(1,128)S(1)}, f32[1,32]{1,0:T(1,128)S(1)}, f32[1,32]{1,0:T(1,128)S(1)}) all-reduce(f32[1,32]{1,0:T(1,128)S(1)} %bitcast.710, f32[1,32]{1,0:T(1,128)S(1)} %bitcast.707, f32[1,32]{1,0:T(1,128)S(1)} %bitcast.705), channel_id=1, replica_groups=mesh['dom'=8,'four'=4] {'dom'}, use_global_device_ids=true, to_apply=%region_49.50 | all-reduce | flops 96 | bytes 768 | tf_op jit(solution)/shard_map/psum | solution.py:220
  (587 shorter events, 465.3 us)
Async XLA Ops:
  5.3 10.8 %copy-start.43 = (s32[1,4]{1,0:T(1,128)S(1)}, s32[1,4]{1,0:T(1,128)}, u32[]{:S(2)}) copy-start(s32[1,4]{1,0:T(1,128)} %param.112) | copy-start | bytes 52
  5.3 10.8 %copy-start.42 = (s32[1,4]{1,0:T(1,128)S(1)}, s32[1,4]{1,0:T(1,128)}, u32[]{:S(2)}) copy-start(s32[1,4]{1,0:T(1,128)} %param.113) | copy-start | bytes 52
  5.3 23.0 %copy-start.44 = (s32[1,4]{1,0:T(1,128)S(1)}, s32[1,4]{1,0:T(1,128)}, u32[]{:S(2)}) copy-start(s32[1,4]{1,0:T(1,128)} %param.114) | copy-start | bytes 52
  10.9 20.9 %all-to-all-start = ((f32[4,1,55296]{2,1,0:T(1,128)}), f32[4,1,55296]{2,1,0:T(1,128)S(1)}, u32[]{:S(2)}, u32[]{:S(2)}) async-start(f32[4,1,55296]{2,1,0:T(1,128)} %reshape.2898), calls=%async_computation | async-start | bytes 1769472 | tf_op jit(solution)/shard_map/all_to_all | solution.py:170
  50.6 34.3 %all-to-all-start.1 = ((f32[6,128,576]{2,0,1:T(8,128)}), f32[6,128,576]{2,0,1:T(8,128)S(1)}, u32[]{:S(2)}, u32[]{:S(2)}) async-start(f32[6,128,576]{2,0,1:T(8,128)} %copy.6841), calls=%async_computation.1 | async-start | bytes 5242880 | tf_op jit(solution)/shard_map/all_to_all | solution.py:173
  60.6 3.2 copy-start.40
  104.5 2.5 copy-start.38
  108.9 3.3 copy-start.41
  112.2 8.1 copy-start.23
  112.2 8.1 copy-start.24
  198.5 0.7 copy-start.33
  199.3 4.2 copy-start.21
  203.5 0.7 copy-start.32
  203.7 79.4 %copy-start.17 = (f32[1,32,48,48]{2,3,1,0:T(8,128)}, f32[1,32,48,48]{2,3,1,0:T(8,128)S(1)}, u32[]{:S(2)}) copy-start(f32[1,32,48,48]{2,3,1,0:T(8,128)S(1)} %get-tuple-element.673) | copy-start | bytes 884740
  278.9 4.2 copy-start.6
  280.7 2.4 copy-start.35
  280.7 2.4 copy-start.36
  288.8 3.0 copy-start.3
  405.3 3.5 copy-start.22
  406.9 2.9 copy-start.8
  412.0 3.0 copy-start
  530.9 5.9 copy-start.20
  530.9 2.6 copy-start.31
  535.2 3.1 copy-start.9
  540.4 2.9 copy-start.1
  641.7 2.6 copy-start.5
  646.2 0.9 copy-start.4
  725.0 2.6 copy-start.16
  764.6 25.4 %copy-start.2 = (f32[1,32,48,48]{2,1,3,0:T(8,128)S(1)}, f32[1,32,48,48]{2,1,3,0:T(8,128)}, u32[]{:S(2)}) copy-start(f32[1,32,48,48]{2,1,3,0:T(8,128)} %constant_dynamic-update-slice_fusion.6) | copy-start | bytes 884740
  793.4 16.8 %copy-start.26 = (f32[1,32,48,48]{2,1,3,0:T(8,128)S(1)}, f32[1,32,48,48]{2,1,3,0:T(8,128)}, u32[]{:S(2)}) copy-start(f32[1,32,48,48]{2,1,3,0:T(8,128)} %get-tuple-element.663) | copy-start | bytes 884740
  810.2 2.5 copy-start.10
  810.2 2.5 copy-start.28
  811.1 5.5 copy-start.18
  820.5 2.0 copy-start.13
  821.0 2.9 copy-start.11
  923.6 2.9 copy-start.29
  923.6 2.9 copy-start.30
  943.1 2.7 copy-start.14
  975.6 23.7 %copy-start.7 = (f32[1,32,48,48]{2,1,3,0:T(8,128)S(1)}, f32[1,32,48,48]{2,1,3,0:T(8,128)}, u32[]{:S(2)}) copy-start(f32[1,32,48,48]{2,1,3,0:T(8,128)} %copy-done.6) | copy-start | bytes 884740
  999.3 3.9 copy-start.12
  999.3 3.9 copy-start.15
  999.4 3.9 copy-start.19
  999.4 3.9 copy-start.25
  999.4 3.9 copy-start.27
  999.4 3.9 copy-start.34
  999.4 3.9 copy-start.37
  1008.9 3.2 copy-start.39
where the time goes:
time: 1030 us; the launch traced here: 1020 us
  blocking collectives  385 us (37%)
  local copies, waits for them, and re-layouts  363 us (35%)
  other arithmetic  185 us (18%)
  matrix products  39.1 us (4%)
  waiting for transfers between devices  21.1 us (2%)
  between operations  16 us (2%)
    all_gather x13, blocking collectives, assemble(): piece = lax.all_gather(packed, 'dom', axis=0, tiled=True)  187 us
    psum x9, blocking collectives, squares(): lax.psum(inner_terms(weight, residual, residual), 'dom')[..., None, None]  128 us
    scatter-add x14, local copies, waits for them, and re-layouts, add_sides(): grid = grid.at[..., -1, :].add(incoming[..., 2, :])  88.5 us
    psum x5, blocking collectives, solve(): lax.psum(inner_terms(weight, direction, image), 'dom')[..., None, None]  69.9 us
    another operation x44, local copies, waits for them, and re-layouts  61.5 us
    another operation x46, local copies, waits for them, and re-layouts, side_values(): jnp.stack([grid[..., 0, :], grid[..., :, -1], grid[..., -1, :], grid[...,...  51.1 us
    scatter-add x13, local copies, waits for them, and re-layouts, add_sides(): grid = grid.at[..., 0, :].add(incoming[..., 0, :])  46.2 us
    another operation x13, other arithmetic, side_values(): jnp.stack([grid[..., 0, :], grid[..., :, -1], grid[..., -1, :], grid[...,...  37.4 us
  transfers between devices with their start and end apart: 2, of which 1 were waited for; matrix products, arithmetic and copies ran while one was open for 1% of the time, Pallas kernels for 0%

commit v1 on v0

--- a/solution.py
+++ b/solution.py
@@ -9,6 +9,11 @@
 REACTION = 2.0
 WAVE_STEP = 0.0625
 HIGHEST = lax.Precision.HIGHEST
+
+
+def summed_here(shard, axis):
+    terms = lax.all_gather(shard, axis)
+    return jnp.sum(terms, axis=0)
 
 
 def gll_tables():
@@ -207,7 +212,7 @@
         return dirichlet_mask * assemble(apply_element(field, rates, weights_line, stiff_block))
 
     def squares(residual):
-        return lax.psum(inner_terms(weight, residual, residual), "dom")[..., None, None]
+        return summed_here(inner_terms(weight, residual, residual), "dom")[..., None, None]
 
     def solve(rhs):
         solution = jnp.zeros_like(rhs)

time: 1030 us -> 1050 us (1.019)
    psum x9 -> x0, blocking collectives: 128 us -> none  [squares(): lax.psum(inner_terms(weight, residual, residual), 'dom')[..., None, None]]
    unnamed x0 -> x9, blocking collectives: none -> 128 us
    unnamed x104 -> x143, local copies, waits for them, and re-layouts: 32.4 us -> 33.8 us
where the time goes in v1:
time: 1050 us; the launch traced here: 1040 us
  blocking collectives  385 us (37%)
  local copies, waits for them, and re-layouts  371 us (35%)
  other arithmetic  186 us (18%)
  matrix products  39.9 us (4%)
  waiting for transfers between devices  29.1 us (3%)
  between operations  16.2 us (2%)
    all_gather x13, blocking collectives, assemble(): piece = lax.all_gather(packed, 'dom', axis=0, tiled=True)  187 us
    unnamed x9, blocking collectives  128 us
    scatter-add x14, local copies, waits for them, and re-layouts, add_sides(): grid = grid.at[..., -1, :].add(incoming[..., 2, :])  88.5 us
    psum x5, blocking collectives, solve(): lax.psum(inner_terms(weight, direction, image), 'dom')[..., None, None]  69.8 us
    another operation x44, local copies, waits for them, and re-layouts  61.1 us
    another operation x46, local copies, waits for them, and re-layouts, side_values(): jnp.stack([grid[..., 0, :], grid[..., :, -1], grid[..., -1, :], grid[...,...  50.6 us
    scatter-add x13, local copies, waits for them, and re-layouts, add_sides(): grid = grid.at[..., 0, :].add(incoming[..., 0, :])  45.8 us
    another operation x13, other arithmetic, side_values(): jnp.stack([grid[..., 0, :], grid[..., :, -1], grid[..., -1, :], grid[...,...  37.5 us
  transfers between devices with their start and end apart: 2, of which 1 were waited for; matrix products, arithmetic and copies ran while one was open for 1% of the time, Pallas kernels for 0%

profile of v1, /device:TPU:0, one launch (start us, length us, event | category | flops | bytes accessed | tf_op | source)
XLA Modules:
  0.0 1036.9 jit_solution(14980765914034609908)
XLA Ops:
  0.6 4.7 copy.6838
  5.3 5.7 reshape.2967
  11.0 5.3 all-to-all-start
  41.3 5.1 reshape.2968
  56.4 4.7 all-to-all-start.1
  63.1 29.1 %all-to-all-done.1 = f32[6,128,576]{2,0,1:T(8,128)} async-done(((f32[6,128,576]{2,0,1:T(8,128)}), f32[6,128,576]{2,0,1:T(8,128)}, u32[]{:S(2)}, u32[]{:S(2)}) %all-to-all-start.1) | async-done | bytes 1769504 | tf_op jit(solution)/shard_map/all_to_all | solution.py:178
  123.0 8.1 fusion.218
  145.8 16.2 %all_gather.111 = f32[8,3,32,192]{3,2,1,0:T(8,128)S(1)} all-gather(f32[1,3,32,192]{3,2,1,0:T(8,128)S(1)} %reshape.2753), channel_id=1, replica_groups=mesh['dom'=8,'four'=4] {'dom'}, dimensions={0}, use_global_device_ids=true | all-gather | bytes 663552 | tf_op jit(solution)/shard_map/all_gather | solution.py:194
  164.5 12.4 %scatter-add.174 = f32[3,32,48,48]{2,3,1,0:T(8,128)S(1)} dynamic-update-slice(f32[3,32,48,48]{2,3,1,0:T(8,128)S(1)} %select_add_fusion, f32[3,32,1,48]{2,3,1,0:T(8,128)} %copy.6860, s32[]{:T(128)} %constant.2451.clone.1, s32[]{:T(128)} %constant.2451.clone.1, s32[]{:T(128)} %constant.2451.clone.1, s32[]{:T(128)} %constant.2451.clone.1) | dynamic-update-slice | bytes 36868 | tf_op jit(solution)/shard_map/scatter-add | solution.py:128
  186.7 19.5 %scatter-add.176 = f32[3,32,48,48]{2,3,1,0:T(8,128)S(1)} dynamic-update-slice(f32[3,32,48,48]{2,3,1,0:T(8,128)S(1)} %scatter-add.175, f32[3,32,1,48]{2,3,1,0:T(8,128)} %copy.6864, s32[]{:T(128)} %constant.2451.clone.1, s32[]{:T(128)} %constant.2451.clone.1, s32[]{:T(128)} %constant.2452.clone.1, s32[]{:T(128)} %constant.2451.clone.1) | dynamic-update-slice | bytes 36868 | tf_op jit(solution)/shard_map/scatter-add | solution.py:130
  223.1 14.3 %all_gather.114 = f32[8,1,32,192]{3,2,1,0:T(8,128)S(1)} all-gather(f32[1,1,32,192]{3,2,1,0:T(8,128)S(1)} %reshape.2759), channel_id=1, replica_groups=mesh['dom'=8,'four'=4] {'dom'}, dimensions={0}, use_global_device_ids=true | all-gather | bytes 221184 | tf_op jit(solution)/shard_map/all_gather | solution.py:194
  245.7 5.3 scatter-add.184
  251.9 17.0 %all-reduce.69 = (f32[256]{0:T(256)S(1)}, f32[32]{0:T(128)S(1)}) all-reduce(f32[256]{0:T(256)S(1)} %dynamic-update-slice.156, f32[32]{0:T(128)S(1)} %get-tuple-element.626), channel_id=2, replica_groups=mesh['dom'=8,'four'=4] {'dom'}, use_global_device_ids=true, to_apply=%add.52 | all-reduce | flops 288 | bytes 2304
  269.7 14.0 %all-reduce.53 = f32[256]{0:T(256)S(1)} all-reduce(f32[256]{0:T(256)S(1)} %dynamic-update-slice.157), channel_id=3, replica_groups=mesh['dom'=8,'four'=4] {'dom'}, use_global_device_ids=true, to_apply=%add.53 | all-reduce | flops 256 | bytes 2048
  307.1 14.2 %all_gather.126 = f32[8,1,32,192]{3,2,1,0:T(8,128)S(1)} all-gather(f32[1,1,32,192]{3,2,1,0:T(8,128)S(1)} %reshape.2783), channel_id=1, replica_groups=mesh['dom'=8,'four'=4] {'dom'}, dimensions={0}, use_global_device_ids=true | all-gather | bytes 221184 | tf_op jit(solution)/shard_map/all_gather | solution.py:194
  331.7 5.3 scatter-add.210
  345.3 14.2 %all_gather.117 = f32[8,1,32,192]{3,2,1,0:T(8,128)S(1)} all-gather(f32[1,1,32,192]{3,2,1,0:T(8,128)S(1)} %reshape.2765), channel_id=1, replica_groups=mesh['dom'=8,'four'=4] {'dom'}, dimensions={0}, use_global_device_ids=true | all-gather | bytes 221184 | tf_op jit(solution)/shard_map/all_gather | solution.py:194
  372.4 5.8 scatter-add.190
  381.6 13.9 %psum.85 = f32[32]{0:T(128)S(1)} all-reduce(f32[32]{0:T(128)S(1)} %get-tuple-element.636), channel_id=1, replica_groups=mesh['dom'=8,'four'=4] {'dom'}, use_global_device_ids=true, to_apply=%region_9.10 | all-reduce | flops 32 | bytes 256 | tf_op jit(solution)/shard_map/psum | solution.py:225
  398.3 13.8 %all-reduce.54 = f32[256]{0:T(256)S(1)} all-reduce(f32[256]{0:T(256)S(1)} %dynamic-update-slice.158), channel_id=4, replica_groups=mesh['dom'=8,'four'=4] {'dom'}, use_global_device_ids=true, to_apply=%add.54 | all-reduce | flops 256 | bytes 2048
  430.7 14.2 %all_gather.138 = f32[8,1,32,192]{3,2,1,0:T(8,128)S(1)} all-gather(f32[1,1,32,192]{3,2,1,0:T(8,128)S(1)} %reshape.2807), channel_id=1, replica_groups=mesh['dom'=8,'four'=4] {'dom'}, dimensions={0}, use_global_device_ids=true | all-gather | bytes 221184 | tf_op jit(solution)/shard_map/all_gather | solution.py:194
  458.1 5.8 scatter-add.236
  472.2 14.2 %all_gather.120 = f32[8,1,32,192]{3,2,1,0:T(8,128)S(1)} all-gather(f32[1,1,32,192]{3,2,1,0:T(8,128)S(1)} %reshape.2771), channel_id=1, replica_groups=mesh['dom'=8,'four'=4] {'dom'}, dimensions={0}, use_global_device_ids=true | all-gather | bytes 221184 | tf_op jit(solution)/shard_map/all_gather | solution.py:194
  496.8 5.3 scatter-add.196
  505.9 13.9 %all-reduce.68 = (f32[256]{0:T(256)S(1)}, f32[32]{0:T(128)S(1)}, f32[32]{0:T(128)S(1)}) all-reduce(f32[256]{0:T(256)S(1)} %dynamic-update-slice.164, f32[32]{0:T(128)S(1)} %get-tuple-element.630, f32[32]{0:T(128)S(1)} %get-tuple-element.635), channel_id=10, replica_groups=mesh['dom'=8,'four'=4] {'dom'}, use_global_device_ids=true, to_apply=%add.60 | all-reduce | flops 320 | bytes 2560
  524.0 13.8 %all-reduce.67 = (f32[256]{0:T(256)S(1)}, f32[256]{0:T(256)S(1)}, f32[256]{0:T(256)S(1)}, f32[32]{0:T(128)S(1)}) all-reduce(f32[256]{0:T(256)S(1)} %dynamic-update-slice.165, f32[256]{0:T(256)S(1)} %dynamic-update-slice.159, f32[256]{0:T(256)S(1)} %dynamic-update-slice.160, ...), channel_id=11, replica_groups=mesh['dom'=8,'four'=4] {'dom'}, use_global_device_ids=true, to_apply=%add.61 | all-reduce | flops 800 | bytes 6400
  562.3 14.4 %all_gather.141 = f32[8,1,32,192]{3,2,1,0:T(8,128)S(1)} all-gather(f32[1,1,32,192]{3,2,1,0:T(8,128)S(1)} %reshape.2813), channel_id=1, replica_groups=mesh['dom'=8,'four'=4] {'dom'}, dimensions={0}, use_global_device_ids=true | all-gather | bytes 221184 | tf_op jit(solution)/shard_map/all_gather | solution.py:194
  589.6 5.8 scatter-add.244
  603.8 14.2 %all_gather.123 = f32[8,1,32,192]{3,2,1,0:T(8,128)S(1)} all-gather(f32[1,1,32,192]{3,2,1,0:T(8,128)S(1)} %reshape.2777), channel_id=1, replica_groups=mesh['dom'=8,'four'=4] {'dom'}, dimensions={0}, use_global_device_ids=true | all-gather | bytes 221184 | tf_op jit(solution)/shard_map/all_gather | solution.py:194
  628.4 5.3 scatter-add.204
  637.9 14.3 %all-reduce.57 = f32[256]{0:T(256)S(1)} all-reduce(f32[256]{0:T(256)S(1)} %dynamic-update-slice.161), channel_id=7, replica_groups=mesh['dom'=8,'four'=4] {'dom'}, use_global_device_ids=true, to_apply=%add.57 | all-reduce | flops 256 | bytes 2048
  666.9 14.2 %all_gather.129 = f32[8,1,32,192]{3,2,1,0:T(8,128)S(1)} all-gather(f32[1,1,32,192]{3,2,1,0:T(8,128)S(1)} %reshape.2789), channel_id=1, replica_groups=mesh['dom'=8,'four'=4] {'dom'}, dimensions={0}, use_global_device_ids=true | all-gather | bytes 221184 | tf_op jit(solution)/shard_map/all_gather | solution.py:194
  694.0 5.8 scatter-add.216
  702.9 13.9 %psum.89 = f32[32]{0:T(128)S(1)} all-reduce(f32[32]{0:T(128)S(1)} %multiply_reduce_fusion.5), channel_id=1, replica_groups=mesh['dom'=8,'four'=4] {'dom'}, use_global_device_ids=true, to_apply=%region_25.26 | all-reduce | flops 32 | bytes 256 | tf_op jit(solution)/shard_map/psum | solution.py:225
  719.7 13.7 %all-reduce.58 = f32[256]{0:T(256)S(1)} all-reduce(f32[256]{0:T(256)S(1)} %dynamic-update-slice.162), channel_id=8, replica_groups=mesh['dom'=8,'four'=4] {'dom'}, use_global_device_ids=true, to_apply=%add.58 | all-reduce | flops 256 | bytes 2048
  751.3 14.2 %all_gather.132 = f32[8,1,32,192]{3,2,1,0:T(8,128)S(1)} all-gather(f32[1,1,32,192]{3,2,1,0:T(8,128)S(1)} %reshape.2795), channel_id=1, replica_groups=mesh['dom'=8,'four'=4] {'dom'}, dimensions={0}, use_global_device_ids=true | all-gather | bytes 221184 | tf_op jit(solution)/shard_map/all_gather | solution.py:194
  777.6 5.8 scatter-add.224
  786.5 13.9 %all-reduce.66 = (f32[32]{0:T(128)S(1)}, f32[32]{0:T(128)S(1)}) all-reduce(f32[32]{0:T(128)S(1)} %get-tuple-element.634, f32[32]{0:T(128)S(1)} %multiply_reduce_fusion.4), channel_id=1, replica_groups=mesh['dom'=8,'four'=4] {'dom'}, use_global_device_ids=true, to_apply=%region_41.42 | all-reduce | flops 64 | bytes 512 | tf_op jit(solution)/shard_map/psum | solution.py:225
  804.3 13.8 %all-reduce.65 = (f32[256]{0:T(256)S(1)}, f32[256]{0:T(256)S(1)}) all-reduce(f32[256]{0:T(256)S(1)} %dynamic-update-slice.166, f32[256]{0:T(256)S(1)} %dynamic-update-slice.163), channel_id=12, replica_groups=mesh['dom'=8,'four'=4] {'dom'}, use_global_device_ids=true, to_apply=%add.62 | all-reduce | flops 512 | bytes 4096
  846.1 14.2 %all_gather.144 = f32[8,1,32,192]{3,2,1,0:T(8,128)S(1)} all-gather(f32[1,1,32,192]{3,2,1,0:T(8,128)S(1)} %reshape.2819), channel_id=1, replica_groups=mesh['dom'=8,'four'=4] {'dom'}, dimensions={0}, use_global_device_ids=true | all-gather | bytes 221184 | tf_op jit(solution)/shard_map/all_gather | solution.py:194
  873.3 5.9 scatter-add.250
  888.9 14.2 %all_gather.135 = f32[8,1,32,192]{3,2,1,0:T(8,128)S(1)} all-gather(f32[1,1,32,192]{3,2,1,0:T(8,128)S(1)} %reshape.2801), channel_id=1, replica_groups=mesh['dom'=8,'four'=4] {'dom'}, dimensions={0}, use_global_device_ids=true | all-gather | bytes 221184 | tf_op jit(solution)/shard_map/all_gather | solution.py:194
  915.5 4.8 scatter-add.230
  926.6 13.9 %psum.94 = f32[32]{0:T(128)S(1)} all-reduce(f32[32]{0:T(128)S(1)} %get-tuple-element.638), channel_id=1, replica_groups=mesh['dom'=8,'four'=4] {'dom'}, use_global_device_ids=true, to_apply=%region_45.46 | all-reduce | flops 32 | bytes 256 | tf_op jit(solution)/shard_map/psum | solution.py:225
  943.6 13.8 %all-reduce.63 = f32[256]{0:T(256)S(1)} all-reduce(f32[256]{0:T(256)S(1)} %dynamic-update-slice.167), channel_id=13, replica_groups=mesh['dom'=8,'four'=4] {'dom'}, use_global_device_ids=true, to_apply=%add.63 | all-reduce | flops 256 | bytes 2048
  973.1 14.2 %all_gather.147 = f32[8,1,32,192]{3,2,1,0:T(8,128)S(1)} all-gather(f32[1,1,32,192]{3,2,1,0:T(8,128)S(1)} %reshape.2825), channel_id=1, replica_groups=mesh['dom'=8,'four'=4] {'dom'}, dimensions={0}, use_global_device_ids=true | all-gather | bytes 221184 | tf_op jit(solution)/shard_map/all_gather | solution.py:194
  995.6 5.3 scatter-add.256
  1002.8 14.1 %all-reduce.64 = (f32[32]{0:T(128)S(1)}, f32[32]{0:T(128)S(1)}, f32[32]{0:T(128)S(1)}) all-reduce(f32[32]{0:T(128)S(1)} %multiply_reduce_fusion, f32[32]{0:T(128)S(1)} %get-tuple-element.637, f32[32]{0:T(128)S(1)} %get-tuple-element.632), channel_id=1, replica_groups=mesh['dom'=8,'four'=4] {'dom'}, use_global_device_ids=true, to_apply=%region_49.50 | all-reduce | flops 96 | bytes 768 | tf_op jit(solution)/shard_map/psum | solution.py:225
  (650 shorter events, 474.7 us)
Async XLA Ops:
  5.3 11.0 %copy-start.35 = (f32[3,32,2304]{2,1,0:T(8,128)S(1)}, f32[3,32,2304]{2,1,0:T(8,128)}, u32[]{:S(2)}) copy-start(f32[3,32,2304]{2,1,0:T(8,128)} %param.111) | copy-start | bytes 2654212
  10.9 6.3 copy-start.48
  10.9 9.6 copy-start.50
  11.0 25.7 %all-to-all-start = ((f32[4,1,55296]{2,1,0:T(1,128)}), f32[4,1,55296]{2,1,0:T(1,128)}, u32[]{:S(2)}, u32[]{:S(2)}) async-start(f32[4,1,55296]{2,1,0:T(1,128)} %reshape.2967), calls=%async_computation | async-start | bytes 1769472 | tf_op jit(solution)/shard_map/all_to_all | solution.py:175
  31.4 2.0 copy-start.49
  56.4 5.3 copy-start.51
  56.4 6.6 copy-start.46
  56.4 35.8 %all-to-all-start.1 = ((f32[6,128,576]{2,0,1:T(8,128)}), f32[6,128,576]{2,0,1:T(8,128)}, u32[]{:S(2)}, u32[]{:S(2)}) async-start(f32[6,128,576]{2,0,1:T(8,128)} %copy.6841), calls=%async_computation.1 | async-start | bytes 5242880 | tf_op jit(solution)/shard_map/all_to_all | solution.py:178
  110.4 4.3 copy-start.45
  113.5 4.8 copy-start.34
  118.3 4.7 copy-start.47
  123.0 8.1 copy-start.29
  123.0 8.1 copy-start.30
  209.1 1.7 copy-start.26
  209.1 1.7 copy-start.37
  209.1 2.5 copy-start.36
  283.8 2.2 copy-start.27
  284.1 5.8 copy-start.6
  286.8 2.4 copy-start.19
  413.8 2.6 copy-start.8
  419.5 2.9 copy-start.1
  539.5 3.7 copy-start.24
  543.2 3.6 copy-start.40
  545.1 2.4 copy-start.9
  545.1 2.4 copy-start.25
  545.2 2.4 copy-start.42
  551.1 2.9 copy-start.2
  652.6 2.6 copy-start.5
  735.1 2.6 copy-start.18
  774.9 25.5 %copy-start.3 = (f32[1,32,48,48]{2,1,3,0:T(8,128)S(1)}, f32[1,32,48,48]{2,1,3,0:T(8,128)}, u32[]{:S(2)}) copy-start(f32[1,32,48,48]{2,1,3,0:T(8,128)} %constant_dynamic-update-slice_fusion.6) | copy-start | bytes 884740
  818.1 2.7 copy-start.32
  820.9 4.3 copy-start.10
  821.7 3.5 copy-start.21
  825.2 3.4 copy-start.43
  825.2 3.4 copy-start.44
  827.0 130.5 %copy-start.11 = (f32[1,32,48,48]{2,3,1,0:T(8,128)}, f32[1,32,48,48]{2,3,1,0:T(8,128)S(1)}, u32[]{:S(2)}) copy-start(f32[1,32,48,48]{2,3,1,0:T(8,128)S(1)} %multiply_add_fusion.2) | copy-start | bytes 884740
  828.6 1.6 copy-start.22
  958.8 2.7 copy-start.16
  962.6 1.8 copy-start.20
  993.2 23.8 %copy-start.7 = (f32[1,32,48,48]{2,1,3,0:T(8,128)S(1)}, f32[1,32,48,48]{2,1,3,0:T(8,128)}, u32[]{:S(2)}) copy-start(f32[1,32,48,48]{2,1,3,0:T(8,128)} %copy-done.6) | copy-start | bytes 884740
  1017.0 3.9 copy-start.14
  1017.0 3.9 copy-start.17
  1017.0 3.9 copy-start.23
  1017.0 3.9 copy-start.31
  1017.0 3.9 copy-start.33
  1017.0 3.9 copy-start.38
  1017.0 3.9 copy-start.39
  1026.5 3.2 copy-start.41
  (6 other events, 8.5 us)
